TPU v7x, 32 devices: a whole 2x2x4 slice. The times are simulated.
32 devices in a mesh: groups: 2 (over x), bricks: 16 (over z, y, core).
Axes of the slice: x: 2, y: 2, z: 4, core: 2. Of those that a mesh axis runs over, the one named last changes fastest.
Arguments:
- snapshots: bfloat16 [512, 32, 32, 256], P(('groups', 'bricks')), parts along dimension 0, may hold values from -30 to 30
- material: int32 [512, 1024], P(('groups', 'bricks')), parts along dimension 0, may hold values from 0 to 15
- occupancy: int32 [32, 4], P(('groups', 'bricks')), parts along dimension 0, may hold values 0 or 1
- moduli: bfloat16 [16], replicated, may hold values from 0.19921875 to 5
Outputs:
- energy_gram: float32 [512, 256], P(('groups', 'bricks')), parts along dimension 0
There are 2 independent parts, one for each index of `groups`. A program takes and returns all parts, laid end to end along the dimension named above; an argument that names none is the same for every part. Nothing has to cross between parts.
All inputs are finite; a program needn't handle non-finite values. No bound on the sum of `occupancy` on one device may be relied on, other than what follows from the above.
Results may differ from a plain program's by a relative error of at most 0.0003.
Values may be sent and summed in bfloat16 or wider, within the bound.
No kernel may reach another device: no remote copies, remote signals or barrier semaphores. Data moves between devices by JAX's collectives and lax.ppermute only.
A program may use at most 128 MiB of HBM per device.

v0:
```python
import jax
import jax.numpy as jnp
from jax import lax
from jax.sharding import PartitionSpec as P


def with_halo(block, sides, width):
    for axis, dim in sides:
        count = lax.axis_size(axis)
        forward = [(i, i + 1) for i in range(count - 1)]
        backward = [(target, source) for source, target in forward]
        low = lax.ppermute(
            lax.slice_in_dim(block, block.shape[dim] - width, None, axis=dim), axis, forward
        )
        high = lax.ppermute(lax.slice_in_dim(block, 0, width, axis=dim), axis, backward)
        block = jnp.concatenate([low, block, high], axis=dim)
    return block


def stencil(padded_field, padded_modulus):
    depth = padded_field.shape[0] - 2
    rows_y = padded_field.shape[1]
    rows_x = padded_field.shape[2]
    field_full = jnp.pad(padded_field, ((0, 0), (1, 1), (1, 1), (0, 0)))
    modulus_full = jnp.pad(padded_modulus, ((0, 0), (1, 1), (1, 1)))
    center = field_full[1 : 1 + depth, 1 : 1 + rows_y, 1 : 1 + rows_x]
    center_mod = modulus_full[1 : 1 + depth, 1 : 1 + rows_y, 1 : 1 + rows_x]
    mod_sum = jnp.zeros_like(center_mod)
    field_sum = jnp.zeros_like(center)
    product_sum = jnp.zeros_like(center)
    total_weight = 0.0
    for shift_z in (-1, 0, 1):
        for shift_y in (-1, 0, 1):
            for shift_x in (-1, 0, 1):
                nonzero = abs(shift_z) + abs(shift_y) + abs(shift_x)
                if nonzero == 0:
                    continue
                weight = (1.0, 0.5, 0.25)[nonzero - 1]
                total_weight = total_weight + weight
                near = field_full[
                    1 + shift_z : 1 + shift_z + depth,
                    1 + shift_y : 1 + shift_y + rows_y,
                    1 + shift_x : 1 + shift_x + rows_x,
                ]
                near_mod = modulus_full[
                    1 + shift_z : 1 + shift_z + depth,
                    1 + shift_y : 1 + shift_y + rows_y,
                    1 + shift_x : 1 + shift_x + rows_x,
                ]
                mod_sum = mod_sum + weight * near_mod
                field_sum = field_sum + weight * near
                product_sum = product_sum + weight * near_mod[..., None] * near
    diagonal = 0.5 * (total_weight * center_mod + mod_sum)
    return (
        diagonal[..., None] * center - 0.5 * center_mod[..., None] * field_sum - 0.5 * product_sum
    )


def local(snapshots, material, occupancy, moduli):
    depth, rows_y, rows_x, width = snapshots.shape
    owners = lax.axis_size("bricks")
    tiles = occupancy.reshape(rows_y // 16, rows_x // 16)
    occupied = jnp.repeat(jnp.repeat(tiles, 16, 0), 16, 1).astype(jnp.bfloat16)
    classes = jnp.arange(moduli.shape[0], dtype=jnp.int32)
    matches = material[..., None] == classes
    looked = jnp.sum(jnp.where(matches, moduli.astype(jnp.float32), 0.0), axis=-1)
    modulus = looked.astype(jnp.bfloat16).reshape(depth, rows_y, rows_x) * occupied[None]
    field = snapshots * occupied[None, :, :, None]
    padded_field, padded_modulus = (
        with_halo(field, (("bricks", 0),), 1),
        with_halo(modulus, (("bricks", 0),), 1),
    )
    image = stencil(padded_field.astype(jnp.float32), padded_modulus.astype(jnp.float32)).astype(
        jnp.bfloat16
    )
    field_flat = field.reshape(-1, width)
    image_flat = image.reshape(-1, width)
    scale = 1.0 / (depth * rows_y * rows_x * owners)
    own_rows = width // owners
    local_gram = lax.dot_general(
        field_flat, image_flat, (((0,), (0,)), ((), ())), preferred_element_type=jnp.float32
    )
    summed = lax.psum(local_gram, "bricks")
    start = lax.axis_index("bricks") * own_rows
    result = lax.dynamic_slice_in_dim(summed, start, own_rows, 0)
    return result * scale


def solution(mesh):
    in_specs = (
        P(("groups", "bricks"), None, None, None),
        P(("groups", "bricks"), None),
        P(("groups", "bricks"), None),
        P(),
    )
    out_specs = P(("groups", "bricks"), None)
    return jax.shard_map(local, mesh=mesh, in_specs=in_specs, out_specs=out_specs, check_vma=False)
```

profile of v0, /device:TPU:1, one launch (start us, length us, event | category | flops | bytes accessed | tf_op | source)
XLA Modules:
  0.0 343.4 jit_solution(14337007187639578546)
XLA Ops:
  6.5 0.0 all-reduce.4.cloned.1.call-start
  6.5 0.7 convert_reduce_fusion
  7.2 0.1 convert_element_type.46
  7.3 0.1 copy.10
  7.4 0.1 broadcast_in_dim.12
  7.5 0.1 convert_element_type.47
  7.6 0.1 copy.11
  7.7 0.7 convert_element_type.49
  8.3 1.1 select_reduce_fusion
  9.5 0.1 convert_element_type.51
  9.7 4.5 %collective-permute-start = (bf16[1,32,32]{2,1,0:T(8,128)(2,1)S(1)}, bf16[1,32,32]{2,1,0:T(8,128)(2,1)S(1)}, u32[]{:S(2)}, u32[]{:S(2)}) collective-permute-start(bf16[1,32,32]{2,1,0:T(8,128)(2,1)S(1)} %get-tuple-element.35), channel_id=1, source_target_pairs={{0,1},{1,2},{2,3},{3,4},{4,5},{5,6},{6,7},{7,8},{8,9},{9,10},{10,1... | collective-permute-start | bytes 6152 | tf_op jit(solution)/shard_map/ppermute | solution.py:12
  14.2 1.9 collective-permute-start.1
  16.1 8.0 %broadcast_multiply_fusion = bf16[16,32,32,256]{3,2,1,0:T(8,128)(2,1)} fusion(bf16[16,32,32,256]{3,2,1,0:T(8,128)(2,1)} %param.4, bf16[32,32]{1,0:T(8,128)(2,1)S(1)} %copy.11), kind=kLoop, calls=%fused_computation.30 | loop fusion | flops 4194304 | bytes 16779264 | tf_op jit(solution)/shard_map/mul | solution.py:68
  24.2 1.3 fusion.31
  25.4 3.6 %collective-permute-start.2 = (bf16[1,32,32,256]{3,2,1,0:T(8,128)(2,1)S(1)}, bf16[1,32,32,256]{3,2,1,0:T(8,128)(2,1)S(1)}, u32[]{:S(2)}, u32[]{:S(2)}) collective-permute-start(bf16[1,32,32,256]{3,2,1,0:T(8,128)(2,1)S(1)} %get-tuple-element.5), channel_id=1, source_target_pairs={{0,1},{1,2},{2,3},{3,4},{4,5},{5,6},{6,7},{7,8},{8,9},{9,10},{10,1... | collective-permute-start | bytes 1572872 | tf_op jit(solution)/shard_map/ppermute | solution.py:12
  29.1 1.9 collective-permute-start.3
  31.0 0.0 collective-permute-done
  31.0 0.0 collective-permute-done.1
  31.1 2.3 fusion.8
  33.4 3.5 %add_multiply_fusion = (f32[16,32,32]{2,1,0:T(8,128)S(1)}, f32[16,32,32]{2,1,0:T(8,128)S(1)}, f32[16,32,32]{2,1,0:T(8,128)S(1)}, f32[16,32,32]{2,1,0:T(8,128)S(1...) fusion(f32[18,32,32]{2,1,0:T(8,128)S(1)} %maximum_convert_fusion.1), kind=kLoop, calls=%fused_computation.78 | loop fusion | flops 966656 | bytes 2129920 | tf_op jit(solution)/shard_map/mul | solution.py:53
  36.9 0.0 collective-permute-done.2
  36.9 2.6 collective-permute-done.3
  39.6 11.4 %maximum_convert_fusion = f32[18,32,32,256]{3,2,1,0:T(8,128)} fusion(bf16[1,32,32,256]{3,2,1,0:T(8,128)(2,1)S(1)} %collective-permute-done.3, bf16[16,32,32,256]{3,2,1,0:T(8,128)(2,1)} %broadcast_multiply_fusion, bf16[1,32,32,256]{3,2,1,0:T(8,128)(2,1)S(1)} %collective-permute-done.2), kind=kLoop, calls=%fused_computation.28 | loop fusion | flops 14155776 | bytes 28311552 | tf_op jit(solution)/shard_map/convert_element_type | solution.py:73
  51.0 184.7 %fusion.37 = bf16[16,32,32,256]{3,2,1,0:T(8,128)(2,1)S(1)} fusion(f32[18,32,32,256]{3,2,1,0:T(8,128)} %maximum_convert_fusion, f32[16,32,32]{2,1,0:T(8,128)} %get-tuple-element.32, f32[16,32,32]{2,1,0:T(8,128)} %get-tuple-element.31, f32[16,32,32]{2,1,0:T(8,128)} %get-tuple-element.30, f32[16,32,32]{2,1,0:T(8,128)} %get-tuple-element.29, ...), kind=kLoop, calls=%fused_computation.27.clone.clone.clone.clone.1 | loop fusion | flops 427819008 | bytes 83951616 | tf_op jit(solution)/shard_map/dot_general | solution.py:80
  235.7 6.5 %fusion.5 = f32[256,256]{1,0:T(8,128)} fusion(bf16[16,32,32,256]{3,2,1,0:T(8,128)(2,1)} %broadcast_multiply_fusion, bf16[16,32,32,256]{3,2,1,0:T(8,128)(2,1)S(1)} %fusion.37), kind=kOutput, calls=%fused_computation.31 | convolution fusion | flops 2147483648 | bytes 17039360 | tf_op jit(solution)/shard_map/dot_general | solution.py:80
  242.1 0.0 all-reduce.4.cloned.1.call-update
  242.2 93.1 %all-reduce.4.cloned.1.call-done = f32[256,256]{1,0:T(8,128)} async-done(((f32[256,256]{1,0:T(8,128)}), f32[256,256]{1,0:T(8,128)}) %all-reduce.4.cloned.1.call-update) | async-done | bytes 262160 | tf_op jit(solution)/shard_map/psum | solution.py:83
  335.2 1.3 dynamic-slice_multiply_fusion
  (4 shorter events, 0.1 us)
Async XLA Ops:
  6.5 328.7 %all-reduce.4.cloned.1.call-start = ((), (), s32[]{:S(2)}) async-start(), calls=%async_computation | async-start | bytes 524288 | tf_op jit(solution)/shard_map/psum | solution.py:83
  9.7 21.4 %collective-permute-start = (bf16[1,32,32]{2,1,0:T(8,128)(2,1)S(1)}, bf16[1,32,32]{2,1,0:T(8,128)(2,1)S(1)}, u32[]{:S(2)}, u32[]{:S(2)}) collective-permute-start(bf16[1,32,32]{2,1,0:T(8,128)(2,1)S(1)} %get-tuple-element.35), channel_id=1, source_target_pairs={{0,1},{1,2},{2,3},{3,4},{4,5},{5,6},{6,7},{7,8},{8,9},{9,10},{10,1... | collective-permute-start | bytes 6152 | tf_op jit(solution)/shard_map/ppermute | solution.py:12
  14.2 16.8 %collective-permute-start.1 = (bf16[1,32,32]{2,1,0:T(8,128)(2,1)S(1)}, bf16[1,32,32]{2,1,0:T(8,128)(2,1)S(1)}, u32[]{:S(2)}, u32[]{:S(2)}) collective-permute-start(bf16[1,32,32]{2,1,0:T(8,128)(2,1)S(1)} %get-tuple-element.36), channel_id=1, source_target_pairs={{1,0},{2,1},{3,2},{4,3},{5,4},{6,5},{7,6},{8,7},{9,8},{10,9},{11,1... | collective-permute-start | bytes 6152 | tf_op jit(solution)/shard_map/ppermute | solution.py:15
  25.4 11.5 %collective-permute-start.2 = (bf16[1,32,32,256]{3,2,1,0:T(8,128)(2,1)S(1)}, bf16[1,32,32,256]{3,2,1,0:T(8,128)(2,1)S(1)}, u32[]{:S(2)}, u32[]{:S(2)}) collective-permute-start(bf16[1,32,32,256]{3,2,1,0:T(8,128)(2,1)S(1)} %get-tuple-element.5), channel_id=1, source_target_pairs={{0,1},{1,2},{2,3},{3,4},{4,5},{5,6},{6,7},{7,8},{8,9},{9,10},{10,1... | collective-permute-start | bytes 1572872 | tf_op jit(solution)/shard_map/ppermute | solution.py:12
  29.1 10.5 %collective-permute-start.3 = (bf16[1,32,32,256]{3,2,1,0:T(8,128)(2,1)S(1)}, bf16[1,32,32,256]{3,2,1,0:T(8,128)(2,1)S(1)}, u32[]{:S(2)}, u32[]{:S(2)}) collective-permute-start(bf16[1,32,32,256]{3,2,1,0:T(8,128)(2,1)S(1)} %get-tuple-element.6), channel_id=1, source_target_pairs={{1,0},{2,1},{3,2},{4,3},{5,4},{6,5},{7,6},{8,7},{9,8},{10,9},{11,1... | collective-permute-start | bytes 1572872 | tf_op jit(solution)/shard_map/ppermute | solution.py:15
Sparse Core Ops, SparseCore 0:
  242.3 92.8 all-reduce.3
where the time goes:
time: 344 us; the launch traced here: 343 us
  other arithmetic  214 us (62%)
  waiting for transfers between devices  95.7 us (28%)
  between operations  13.5 us (4%)
  starting transfers between devices  12 us (3%)
  matrix products  6.48 us (2%)
    dot_general x1, other arithmetic, local(): lax.dot_general(field_flat, image_flat, (((0,), (0,)), ((), ())), preferr...  185 us
    psum x1, waiting for transfers between devices, local(): summed = lax.psum(local_gram, 'bricks')  93.1 us
    convert_element_type x1, other arithmetic, local(): padded_field.astype(jnp.float32)  11.4 us
    ppermute x2, starting transfers between devices, with_halo(): lax.ppermute(lax.slice_in_dim(block, block.shape[dim] - width, None, axis...  8.18 us
    mul x1, other arithmetic, local(): field = snapshots * occupied[None, :, :, None]  8.04 us
  transfers between devices with their start and end apart: 5, of which 2 were waited for; matrix products, arithmetic and copies ran while one was open for 4% of the time, Pallas kernels for 0%

commit v1 on v0

--- a/solution.py
+++ b/solution.py
@@ -80,7 +80,7 @@
     local_gram = lax.dot_general(
         field_flat, image_flat, (((0,), (0,)), ((), ())), preferred_element_type=jnp.float32
     )
-    summed = lax.psum(local_gram, "bricks")
+    summed = jnp.sum(lax.all_gather(local_gram, "bricks"), axis=0)
     start = lax.axis_index("bricks") * own_rows
     result = lax.dynamic_slice_in_dim(summed, start, own_rows, 0)
     return result * scale

time: 344 us -> 307 us (0.89)
  waiting for transfers between devices: 95.7 us -> 57.3 us
    psum x1 -> x0, waiting for transfers between devices: 93.1 us -> none  [local(): summed = lax.psum(local_gram, 'bricks')]
    all_gather x0 -> x1, waiting for transfers between devices: none -> 54.6 us  [local(): summed = jnp.sum(lax.all_gather(local_gram, 'bricks'), axis=0)]
  transfers between devices with their start and end apart: 5 -> 5, of which waited for: 2 -> 2; matrix products, arithmetic and copies ran while one was open for 4% -> 5% of each run, Pallas kernels for 0% -> 0%
where the time goes in v1:
time: 307 us
  other arithmetic  216 us (70%)
  waiting for transfers between devices  57.3 us (19%)
  between operations  13.5 us (4%)
  starting transfers between devices  12 us (4%)
  matrix products  6.48 us (2%)
    dot_general x1, other arithmetic, local(): lax.dot_general(field_flat, image_flat, (((0,), (0,)), ((), ())), preferr...  185 us
    all_gather x1, waiting for transfers between devices, local(): summed = jnp.sum(lax.all_gather(local_gram, 'bricks'), axis=0)  54.6 us
    convert_element_type x1, other arithmetic, local(): padded_field.astype(jnp.float32)  11.4 us
    ppermute x2, starting transfers between devices, with_halo(): lax.ppermute(lax.slice_in_dim(block, block.shape[dim] - width, None, axis...  8.18 us
    mul x1, other arithmetic, local(): field = snapshots * occupied[None, :, :, None]  8.04 us
    dot_general x1, matrix products, local(): lax.dot_general(field_flat, image_flat, (((0,), (0,)), ((), ())), preferr...  6.48 us
  transfers between devices with their start and end apart: 5, of which 2 were waited for; matrix products, arithmetic and copies ran while one was open for 5% of the time, Pallas kernels for 0%

profile of v1, /device:TPU:1, one launch (start us, length us, event | category | flops | bytes accessed | tf_op | source)
XLA Modules:
  0.0 306.7 jit_solution(3546975770627629443)
XLA Ops:
  6.5 0.0 all-gather.3.cloned.1.call-start
  6.5 0.7 convert_reduce_fusion
  7.2 0.1 convert_element_type.46
  7.3 0.1 copy.10
  7.4 0.1 broadcast_in_dim.12
  7.5 0.1 convert_element_type.47
  7.6 0.1 copy.11
  7.7 0.7 convert_element_type.49
  8.3 1.1 select_reduce_fusion
  9.5 0.1 convert_element_type.51
  9.7 4.5 %collective-permute-start = (bf16[1,32,32]{2,1,0:T(8,128)(2,1)S(1)}, bf16[1,32,32]{2,1,0:T(8,128)(2,1)S(1)}, u32[]{:S(2)}, u32[]{:S(2)}) collective-permute-start(bf16[1,32,32]{2,1,0:T(8,128)(2,1)S(1)} %get-tuple-element.35), channel_id=1, source_target_pairs={{0,1},{1,2},{2,3},{3,4},{4,5},{5,6},{6,7},{7,8},{8,9},{9,10},{10,1... | collective-permute-start | bytes 6152 | tf_op jit(solution)/shard_map/ppermute | solution.py:12
  14.2 1.9 collective-permute-start.1
  16.1 8.0 %broadcast_multiply_fusion = bf16[16,32,32,256]{3,2,1,0:T(8,128)(2,1)} fusion(bf16[16,32,32,256]{3,2,1,0:T(8,128)(2,1)} %param.4, bf16[32,32]{1,0:T(8,128)(2,1)S(1)} %copy.11), kind=kLoop, calls=%fused_computation.30 | loop fusion | flops 4194304 | bytes 16779264 | tf_op jit(solution)/shard_map/mul | solution.py:68
  24.2 1.3 fusion.31
  25.4 3.6 %collective-permute-start.2 = (bf16[1,32,32,256]{3,2,1,0:T(8,128)(2,1)S(1)}, bf16[1,32,32,256]{3,2,1,0:T(8,128)(2,1)S(1)}, u32[]{:S(2)}, u32[]{:S(2)}) collective-permute-start(bf16[1,32,32,256]{3,2,1,0:T(8,128)(2,1)S(1)} %get-tuple-element.5), channel_id=1, source_target_pairs={{0,1},{1,2},{2,3},{3,4},{4,5},{5,6},{6,7},{7,8},{8,9},{9,10},{10,1... | collective-permute-start | bytes 1572872 | tf_op jit(solution)/shard_map/ppermute | solution.py:12
  29.1 1.9 collective-permute-start.3
  31.0 0.0 collective-permute-done
  31.0 0.0 collective-permute-done.1
  31.1 2.3 fusion.8
  33.4 3.5 %add_multiply_fusion = (f32[16,32,32]{2,1,0:T(8,128)S(1)}, f32[16,32,32]{2,1,0:T(8,128)S(1)}, f32[16,32,32]{2,1,0:T(8,128)S(1)}, f32[16,32,32]{2,1,0:T(8,128)S(1...) fusion(f32[18,32,32]{2,1,0:T(8,128)S(1)} %maximum_convert_fusion.1), kind=kLoop, calls=%fused_computation.78 | loop fusion | flops 966656 | bytes 2129920 | tf_op jit(solution)/shard_map/mul | solution.py:53
  36.9 0.0 collective-permute-done.2
  36.9 2.6 collective-permute-done.3
  39.6 11.4 %maximum_convert_fusion = f32[18,32,32,256]{3,2,1,0:T(8,128)} fusion(bf16[1,32,32,256]{3,2,1,0:T(8,128)(2,1)S(1)} %collective-permute-done.3, bf16[16,32,32,256]{3,2,1,0:T(8,128)(2,1)} %broadcast_multiply_fusion, bf16[1,32,32,256]{3,2,1,0:T(8,128)(2,1)S(1)} %collective-permute-done.2), kind=kLoop, calls=%fused_computation.28 | loop fusion | flops 14155776 | bytes 28311552 | tf_op jit(solution)/shard_map/convert_element_type | solution.py:73
  51.0 184.7 %fusion.37 = bf16[16,32,32,256]{3,2,1,0:T(8,128)(2,1)S(1)} fusion(f32[18,32,32,256]{3,2,1,0:T(8,128)} %maximum_convert_fusion, f32[16,32,32]{2,1,0:T(8,128)} %get-tuple-element.32, f32[16,32,32]{2,1,0:T(8,128)} %get-tuple-element.31, f32[16,32,32]{2,1,0:T(8,128)} %get-tuple-element.30, f32[16,32,32]{2,1,0:T(8,128)} %get-tuple-element.29, ...), kind=kLoop, calls=%fused_computation.27.clone.clone.clone.clone.1 | loop fusion | flops 427819008 | bytes 83951616 | tf_op jit(solution)/shard_map/dot_general | solution.py:80
  235.7 6.5 %fusion.5 = f32[256,256]{1,0:T(8,128)} fusion(bf16[16,32,32,256]{3,2,1,0:T(8,128)(2,1)} %broadcast_multiply_fusion, bf16[16,32,32,256]{3,2,1,0:T(8,128)(2,1)S(1)} %fusion.37), kind=kOutput, calls=%fused_computation.31 | convolution fusion | flops 2147483648 | bytes 17039360 | tf_op jit(solution)/shard_map/dot_general | solution.py:80
  242.1 0.0 all-gather.3.cloned.1.call-update
  242.2 54.6 %all-gather.3.cloned.1.call-done = f32[4096,256]{1,0:T(8,128)} async-done(((f32[256,256]{1,0:T(8,128)}), f32[4096,256]{1,0:T(8,128)}) %all-gather.3.cloned.1.call-update) | async-done | bytes 4194320 | tf_op jit(solution)/shard_map/all_gather | solution.py:83
  296.8 2.5 reduce_sum.19
  299.2 0.6 dynamic-slice_multiply_fusion
  (4 shorter events, 0.1 us)
Async XLA Ops:
  6.5 290.2 %all-gather.3.cloned.1.call-start = ((), (), s32[]{:S(2)}) async-start(), calls=%async_computation | async-start | bytes 4456448 | tf_op jit(solution)/shard_map/all_gather | solution.py:83
  9.7 21.4 %collective-permute-start = (bf16[1,32,32]{2,1,0:T(8,128)(2,1)S(1)}, bf16[1,32,32]{2,1,0:T(8,128)(2,1)S(1)}, u32[]{:S(2)}, u32[]{:S(2)}) collective-permute-start(bf16[1,32,32]{2,1,0:T(8,128)(2,1)S(1)} %get-tuple-element.35), channel_id=1, source_target_pairs={{0,1},{1,2},{2,3},{3,4},{4,5},{5,6},{6,7},{7,8},{8,9},{9,10},{10,1... | collective-permute-start | bytes 6152 | tf_op jit(solution)/shard_map/ppermute | solution.py:12
  14.2 16.8 %collective-permute-start.1 = (bf16[1,32,32]{2,1,0:T(8,128)(2,1)S(1)}, bf16[1,32,32]{2,1,0:T(8,128)(2,1)S(1)}, u32[]{:S(2)}, u32[]{:S(2)}) collective-permute-start(bf16[1,32,32]{2,1,0:T(8,128)(2,1)S(1)} %get-tuple-element.36), channel_id=1, source_target_pairs={{1,0},{2,1},{3,2},{4,3},{5,4},{6,5},{7,6},{8,7},{9,8},{10,9},{11,1... | collective-permute-start | bytes 6152 | tf_op jit(solution)/shard_map/ppermute | solution.py:15
  25.4 11.5 %collective-permute-start.2 = (bf16[1,32,32,256]{3,2,1,0:T(8,128)(2,1)S(1)}, bf16[1,32,32,256]{3,2,1,0:T(8,128)(2,1)S(1)}, u32[]{:S(2)}, u32[]{:S(2)}) collective-permute-start(bf16[1,32,32,256]{3,2,1,0:T(8,128)(2,1)S(1)} %get-tuple-element.5), channel_id=1, source_target_pairs={{0,1},{1,2},{2,3},{3,4},{4,5},{5,6},{6,7},{7,8},{8,9},{9,10},{10,1... | collective-permute-start | bytes 1572872 | tf_op jit(solution)/shard_map/ppermute | solution.py:12
  29.1 10.5 %collective-permute-start.3 = (bf16[1,32,32,256]{3,2,1,0:T(8,128)(2,1)S(1)}, bf16[1,32,32,256]{3,2,1,0:T(8,128)(2,1)S(1)}, u32[]{:S(2)}, u32[]{:S(2)}) collective-permute-start(bf16[1,32,32,256]{3,2,1,0:T(8,128)(2,1)S(1)} %get-tuple-element.6), channel_id=1, source_target_pairs={{1,0},{2,1},{3,2},{4,3},{5,4},{6,5},{7,6},{8,7},{9,8},{10,9},{11,1... | collective-permute-start | bytes 1572872 | tf_op jit(solution)/shard_map/ppermute | solution.py:15
Sparse Core Ops, SparseCore 0:
  242.3 54.4 all-gather.2
